TPU v7x, 32 devices: a whole 2x2x4 slice. The times are simulated.
32 devices in a mesh: dom: 32 (over z, y, x, core).
Axes of the slice: x: 2, y: 2, z: 4, core: 2. Of those that a mesh axis runs over, the one named last changes fastest.
Arguments:
- features: bfloat16 [262144, 128], P('dom'), may hold values from -6 to 6
- labels: int32 [65536], P('dom'), may hold values from 0 to 171
- seed_count: int32 [32], P('dom'), may hold values from 1024 to 2048, as said below
- src1: int32 [65536, 15], P('dom'), may hold values from -1 to 8191, as said below
- cnt1: int32 [65536], P('dom'), may hold values from 0 to 15, as said below
- dst1: int32 [65536], P('dom'), may hold values from 0 to 8191
- src2: int32 [16384, 10], P('dom'), may hold values from -1 to 8191, as said below
- cnt2: int32 [16384], P('dom'), may hold values from 0 to 10, as said below
- dst2: int32 [16384], P('dom'), may hold values from 0 to 2047
- master: float32 [155648], P('dom')
- moment1: float32 [155648], P('dom'), may hold values from -0.046875 to 0.046875
- moment2: float32 [155648], P('dom'), may hold values from 1e-06 to 0.0001
Outputs:
- loss: float32 [], replicated
- new_master: float32 [155648], P('dom')
- new_moment1: float32 [155648], P('dom')
- new_moment2: float32 [155648], P('dom')
Inputs may be any that keep to these rules, and one draw needn't show every extreme that they name: `seed_count`: each trainer has between 1024 and 2048 live seeds; some trainer has exactly 2048. `src1`: in each slot the first cnt entries are source rows and the rest are -1; an empty slot has all -1; some slot is full. From one owner to one device at most 32 slots are non-empty, and some owner sends exactly 32 to some device; which slots are non-empty varies. `cnt1`: equals the number of non-negative entries of the matching src1 slot. `src2`: in each slot the first cnt entries are source rows and the rest are -1; an empty slot has all -1; some slot is full. From one owner to one trainer at most 8 slots are non-empty, and some owner sends exactly 8 to some trainer; which slots are non-empty varies. `cnt2`: equals the number of non-negative entries of the matching src2 slot.
All inputs are finite; a program needn't handle non-finite values.
Results may differ from a plain program's by a relative error of at most 0.00035.
The roundings to bfloat16 on the way count: a program that leaves them out, or rounds other values in their place, can miss the bound.
Values may be sent and summed in bfloat16 or wider, within the bound.
No kernel may reach another device: no remote copies, remote signals or barrier semaphores. Data moves between devices by JAX's collectives and lax.ppermute only.
A program may use at most 128 MiB of HBM per device.

v0:
```python
import jax
import jax.numpy as jnp
from jax import lax
from jax.sharding import PartitionSpec as P

F = 128
H = 256
C = 172
STEP = 4
SEEDS = 2048
MID = 8192
CAP1 = 64
CAP2 = 16


learn_rate = 0.02
weight_decay = 0.01
adam_eps = 1e-08


def partial_sums(source_rows, sources):
    present = (sources >= 0).astype(source_rows.dtype)
    picked = source_rows[jnp.maximum(sources, 0)]
    return jnp.einsum("sf,sfw->sw", present, picked, preferred_element_type=jnp.float32)


def neighbour_sums(received, targets, counts, groups):
    totals = jax.ops.segment_sum(received.astype(jnp.float32), targets, groups)
    degree = jnp.maximum(jax.ops.segment_sum(counts, targets, groups), 1).astype(jnp.float32)
    return (totals, degree)


def body(
    features, labels, seed_count, src1, cnt1, dst1, src2, cnt2, dst2, master, moment1, moment2
):
    devices = lax.axis_size("dom")
    weights_flat = lax.all_gather(master.astype(jnp.bfloat16), "dom", axis=0, tiled=True)
    first_end = 2 * F * H
    second_end = first_end + 2 * H * C
    w_first = weights_flat[:first_end].reshape(2, F, H)
    w_second = weights_flat[first_end:second_end].reshape(2, H, C)
    bias_one = weights_flat[second_end : second_end + H].astype(jnp.float32)
    bias_two = weights_flat[second_end + H : second_end + H + C].astype(jnp.float32)
    outgoing_one = partial_sums(features, src1).astype(jnp.bfloat16).reshape(devices, CAP1, F)
    incoming_one = lax.all_to_all(
        outgoing_one, "dom", split_axis=0, concat_axis=0, tiled=True
    ).reshape(-1, F)
    targets_one, counts_one = (dst1, cnt1)
    sums_one, degree_one = neighbour_sums(incoming_one, targets_one, counts_one, MID)
    means_one = (sums_one / degree_one[:, None]).astype(jnp.bfloat16)
    z_one = (
        jnp.dot(features, w_first[0], preferred_element_type=jnp.float32)
        + jnp.dot(means_one, w_first[1], preferred_element_type=jnp.float32)
        + bias_one
    )
    hidden = jax.nn.relu(z_one).astype(jnp.bfloat16)
    outgoing_two = partial_sums(hidden, src2).astype(jnp.bfloat16).reshape(devices, CAP2, H)
    incoming_two = lax.all_to_all(
        outgoing_two, "dom", split_axis=0, concat_axis=0, tiled=True
    ).reshape(-1, H)
    targets_two, counts_two, sources_two = (dst2, cnt2, src2)
    sums_two, degree_two = neighbour_sums(incoming_two, targets_two, counts_two, SEEDS)
    means_two = (sums_two / degree_two[:, None]).astype(jnp.bfloat16)
    self_rows = hidden[:SEEDS]
    logits = (
        jnp.dot(self_rows, w_second[0], preferred_element_type=jnp.float32)
        + jnp.dot(means_two, w_second[1], preferred_element_type=jnp.float32)
        + bias_two
    )
    valid_mask = (jnp.arange(SEEDS, dtype=jnp.int32) < seed_count[0]).astype(jnp.float32)
    target = (labels[:, None] == jnp.arange(C, dtype=jnp.int32)[None, :]).astype(jnp.float32)
    row_loss = (
        jax.nn.logsumexp(logits, axis=1)
        - 0.9 * jnp.sum(logits * target, 1)
        - 0.1 * jnp.mean(logits, 1)
    )
    loss_sum, seed_total = lax.psum(
        (jnp.sum(row_loss * valid_mask), seed_count[0].astype(jnp.float32)), "dom"
    )
    loss_value = loss_sum / seed_total
    grad_logits = (
        (jax.nn.softmax(logits, axis=1) - 0.9 * target - 0.1 / C)
        * (valid_mask / seed_total)[:, None]
    ).astype(jnp.bfloat16)
    grad_self_two = jnp.einsum(
        "nh,nc->hc", self_rows, grad_logits, preferred_element_type=jnp.float32
    )
    grad_neigh_two = jnp.einsum(
        "nh,nc->hc", means_two, grad_logits, preferred_element_type=jnp.float32
    )
    grad_bias_two = jnp.sum(grad_logits.astype(jnp.float32), 0)
    d_self = jnp.einsum("nc,hc->nh", grad_logits, w_second[0], preferred_element_type=jnp.float32)
    d_means = jnp.einsum("nc,hc->nh", grad_logits, w_second[1], preferred_element_type=jnp.float32)
    d_sums = (d_means / degree_two[:, None]).astype(jnp.bfloat16)
    returning = d_sums[targets_two].reshape(devices, CAP2, H)
    slot_grads = lax.all_to_all(returning, "dom", split_axis=0, concat_axis=0, tiled=True).reshape(
        -1, H
    )
    present_two = (sources_two >= 0).astype(jnp.bfloat16)
    spread = (present_two[:, :, None] * slot_grads[:, None, :]).astype(jnp.float32).reshape(-1, H)
    d_hidden = jax.ops.segment_sum(spread, jnp.maximum(sources_two, 0).reshape(-1), MID)
    d_hidden = d_hidden.at[:SEEDS].add(d_self)
    d_z_one = d_hidden.astype(jnp.bfloat16) * (z_one > 0).astype(jnp.bfloat16)
    grad_self_one = jnp.einsum("nf,nh->fh", features, d_z_one, preferred_element_type=jnp.float32)
    grad_neigh_one = jnp.einsum("nf,nh->fh", means_one, d_z_one, preferred_element_type=jnp.float32)
    grad_bias_one = jnp.sum(d_z_one.astype(jnp.float32), 0)
    tail_len = weights_flat.shape[0] - second_end - H - C
    local_grad = jnp.concatenate(
        [
            jnp.stack([grad_self_one, grad_neigh_one]).reshape(-1),
            jnp.stack([grad_self_two, grad_neigh_two]).reshape(-1),
            grad_bias_one,
            grad_bias_two,
            jnp.zeros((tail_len,), jnp.float32),
        ]
    )
    gradient = lax.psum_scatter(local_grad, "dom", scatter_dimension=0, tiled=True)
    new_first = 0.5 * moment1 + 0.5 * gradient
    new_second = 0.5 * moment2 + 0.5 * gradient * gradient
    correction = 1.0 - 0.5**STEP
    new_master = master - learn_rate * (
        new_first / correction / (jnp.sqrt(new_second / correction) + adam_eps)
        + weight_decay * master
    )
    return (loss_value, new_master, new_first, new_second)


def solution(mesh):
    placed = (
        P("dom", None),
        P("dom"),
        P("dom"),
        P("dom", None),
        P("dom"),
        P("dom"),
        P("dom", None),
        P("dom"),
        P("dom"),
        P("dom"),
        P("dom"),
        P("dom"),
    )
    return jax.shard_map(
        body,
        mesh=mesh,
        in_specs=placed,
        out_specs=(P(), P("dom"), P("dom"), P("dom")),
        check_vma=False,
    )
```

profile of v0, /device:TPU:0, one launch (start us, length us, event | category | flops | bytes accessed | tf_op | source)
XLA Modules:
  0.0 572.2 jit_solution(17336279825595590667)
XLA Ops:
  10.2 107.0 %gather_fusion = bf16[30720,128]{1,0:T(8,128)(2,1)} fusion(bf16[8192,128]{1,0:T(8,128)(2,1)S(1)} %copy-done, s32[30720]{0:T(1024)S(1)} %broadcast_clamp_fusion), kind=kCustom, calls=%fused_computation | custom fusion | bytes 15851520 | tf_op jit(solution)/shard_map/gather | solution.py:23
  117.2 12.5 %reshape.117 = bf16[2048,15,128]{2,1,0:T(8,128)(2,1)} reshape(bf16[30720,128]{1,0:T(8,128)(2,1)} %gather_fusion) | data formatting | bytes 15728640 | tf_op jit(solution)/shard_map/gather | solution.py:23
  131.5 5.7 fusion.31
  138.1 7.3 %all-to-all-start = ((bf16[32,64,128]{2,1,0:T(8,128)(2,1)}), bf16[32,64,128]{2,1,0:T(8,128)(2,1)S(1)}, u32[]{:S(2)}, u32[]{:S(2)}) async-start(bf16[32,64,128]{2,1,0:T(8,128)(2,1)} %bitcast.4), calls=%async_computation | async-start | bytes 1048576 | tf_op jit(solution)/shard_map/all_to_all | solution.py:45
  145.5 45.8 %all-gather = bf16[32,1,4864]{2,1,0:T(2,128)(2,1)S(1)} all-gather(bf16[1,1,4864]{2,1,0:T(2,128)(2,1)S(1)} %reshape.190), channel_id=1, replica_groups=mesh['dom'=32] {'dom'}, dimensions={0}, use_global_device_ids=true | all-gather | bytes 321024 | tf_op jit(solution)/shard_map/all_gather | solution.py:37
  197.0 3.4 scatter_custom_fusion.3
  202.9 11.6 %scatter_custom_fusion.1 = s32[8192]{0:T(1024)S(1)} fusion(s32[2048]{0:T(1024)} %param.19, s32[2048]{0:T(1024)} %param.18, s32[]{:T(128)} %constant.71.clone.1), kind=kCustom, calls=%fused_computation.60 | custom fusion | flops 2048 | bytes 33280 | tf_op jit(solution)/shard_map/scatter-add | solution.py:29
  215.1 5.3 fusion.30
  220.4 13.8 %scatter_custom_fusion = f32[8192,128]{1,0:T(8,128)} fusion(s32[2048]{0:T(1024)} %param.19, f32[]{:T(128)} %constant.70.clone.1, bf16[2048,128]{1,0:T(8,128)(2,1)S(1)} %bitcast.54), kind=kCustom, calls=%fused_computation.25 | custom fusion | flops 524288 | bytes 4719104 | tf_op jit(solution)/shard_map/scatter-add | solution.py:28
  237.1 10.0 %maximum_convert_fusion = (bf16[8192,256]{1,0:T(8,128)(2,1)}, f32[8192,256]{1,0:T(8,128)}) fusion(f32[256]{0:T(256)S(1)} %slice_convert_fusion.1, f32[8192,256]{1,0:T(8,128)} %fusion.30, bf16[8192,128]{1,0:T(8,128)(2,1)S(1)} %divide_convert_fusion, bf16[128,256]{1,0:T(8,128)(2,1)S(1)} %slice.79), kind=kOutput, calls=%fused_computation.11 | convolution fusion | flops 545259520 | bytes 23135232 | tf_op jit(solution)/shard_map/dot_general | solution.py:53
  247.1 22.4 %gather_fusion.1 = bf16[5120,256]{1,0:T(8,128)(2,1)} fusion(bf16[8192,256]{1,0:T(8,128)(2,1)} %get-tuple-element.35, s32[5120]{0:T(1024)S(1)} %broadcast_clamp_fusion.1), kind=kCustom, calls=%fused_computation.1 | custom fusion | bytes 5263360 | tf_op jit(solution)/shard_map/gather | solution.py:23
  269.5 5.9 %reshape.125 = bf16[512,10,256]{2,1,0:T(8,128)(2,1)} reshape(bf16[5120,256]{1,0:T(8,128)(2,1)} %gather_fusion.1) | data formatting | bytes 5242880 | tf_op jit(solution)/shard_map/gather | solution.py:23
  285.3 7.1 %all-to-all-done.1 = bf16[32,16,256]{2,1,0:T(8,128)(2,1)S(1)} async-done(((bf16[32,16,256]{2,1,0:T(8,128)(2,1)}), bf16[32,16,256]{2,1,0:T(8,128)(2,1)S(1)}, u32[]{:S(2)}, u32[]{:S(2)}) %all-to-all-start.1) | async-done | bytes 262176 | tf_op jit(solution)/shard_map/all_to_all | solution.py:58
  292.4 5.1 scatter_custom_fusion.2
  303.9 38.7 %all-reduce.1 = (f32[]{:T(128)}, f32[]{:T(128)}) all-reduce(f32[]{:T(128)} %select_reduce_fusion.1, f32[]{:T(128)S(6)} %convert_element_type.85), channel_id=1, replica_groups=mesh['dom'=32] {'dom'}, use_global_device_ids=true, to_apply=%region_9.10 | all-reduce | flops 2 | bytes 16 | tf_op jit(solution)/shard_map/psum | solution.py:77
  348.6 3.6 gather_fusion.2
  352.3 4.0 all-to-all-start.2
  360.3 6.6 %all-to-all-done.2 = bf16[32,16,256]{2,1,0:T(8,128)(2,1)} async-done(((bf16[32,16,256]{2,1,0:T(8,128)(2,1)}), bf16[32,16,256]{2,1,0:T(8,128)(2,1)}, u32[]{:S(2)}, u32[]{:S(2)}) %all-to-all-start.2) | async-done | bytes 262176 | tf_op jit(solution)/shard_map/all_to_all | solution.py:96
  370.1 6.1 %mul.98 = bf16[5120,256]{1,0:T(8,128)(2,1)} reshape(bf16[512,10,256]{2,1,0:T(8,128)(2,1)} %mul.97) | data formatting | bytes 5242880 | tf_op jit(solution)/shard_map/mul | solution.py:100
  376.3 37.6 %scatter_custom_fusion.4 = f32[8192,256]{1,0:T(8,128)} fusion(s32[5120]{0:T(1024)} %copy-done.10, f32[]{:T(128)} %constant.70.clone.1, bf16[5120,256]{1,0:T(8,128)(2,1)} %mul.98, bf16[5120]{0:T(1024)(128)(2,1)S(1)} %copy-done.13), kind=kCustom, calls=%fused_computation.13 | custom fusion | flops 3932160 | bytes 11020800 | tf_op jit(solution)/shard_map/scatter-add | solution.py:101
  413.9 3.5 fusion.4
  417.4 7.3 %convert_reduce_fusion = (f32[256]{0:T(256)S(1)}, bf16[8192,256]{1,0:T(8,128)(2,1)S(1)}) fusion(f32[8192,256]{1,0:T(8,128)} %fusion.4, f32[8192,256]{1,0:T(8,128)} %get-tuple-element.36), kind=kLoop, calls=%fused_computation.10 | loop fusion | flops 10485504 | bytes 20972544 | tf_op jit(solution)/shard_map/reduce_sum | solution.py:106
  429.8 5.5 concatenate.5
  436.5 125.8 %all-reduce.4.cloned.1.call-done = f32[155648]{0:T(1024)} async-done(((f32[155648]{0:T(1024)}), f32[155648]{0:T(1024)}) %all-reduce.4.cloned.1.call-update) | async-done | bytes 622608
  (104 shorter events, 51.8 us)
Async XLA Ops:
  7.2 3.0 copy-start
  137.2 8.2 %copy-start.11 = (f32[4864]{0:T(1024)S(1)}, f32[4864]{0:T(1024)}, u32[]{:S(2)}) copy-start(f32[4864]{0:T(1024)} %param.23) | copy-start | bytes 58372
  138.1 82.3 %all-to-all-start = ((bf16[32,64,128]{2,1,0:T(8,128)(2,1)}), bf16[32,64,128]{2,1,0:T(8,128)(2,1)S(1)}, u32[]{:S(2)}, u32[]{:S(2)}) async-start(bf16[32,64,128]{2,1,0:T(8,128)(2,1)} %bitcast.4), calls=%async_computation | async-start | bytes 1048576 | tf_op jit(solution)/shard_map/all_to_all | solution.py:45
  193.1 3.9 copy-start.20
  196.1 86.3 %copy-start.7 = (bf16[256,172]{1,0:T(8,128)(2,1)}, bf16[256,172]{1,0:T(8,128)(2,1)S(1)}, u32[]{:S(2)}) copy-start(bf16[256,172]{1,0:T(8,128)(2,1)S(1)} %squeeze.7) | copy-start | bytes 264196
  196.5 23.9 %copy-start.10 = (s32[5120]{0:T(1024)}, s32[5120]{0:T(1024)S(1)}, u32[]{:S(2)}) copy-start(s32[5120]{0:T(1024)S(1)} %reshape.126) | copy-start | bytes 61444
  200.4 97.1 %copy-start.15 = (f32[2048]{0:T(1024)}, f32[2048]{0:T(1024)S(1)}, u32[]{:S(2)}) copy-start(f32[2048]{0:T(1024)S(1)} %maximum_convert_fusion.2) | copy-start | bytes 24580
  237.1 10.0 %copy-start.1 = (bf16[8192,128]{1,0:T(8,128)(2,1)}, bf16[8192,128]{1,0:T(8,128)(2,1)S(1)}, u32[]{:S(2)}) copy-start(bf16[8192,128]{1,0:T(8,128)(2,1)S(1)} %divide_convert_fusion) | copy-start | bytes 6291460
  279.2 13.2 %all-to-all-start.1 = ((bf16[32,16,256]{2,1,0:T(8,128)(2,1)}), bf16[32,16,256]{2,1,0:T(8,128)(2,1)S(1)}, u32[]{:S(2)}, u32[]{:S(2)}) async-start(bf16[32,16,256]{2,1,0:T(8,128)(2,1)} %bitcast.8), calls=%async_computation.1 | async-start | bytes 524288 | tf_op jit(solution)/shard_map/all_to_all | solution.py:58
  297.5 2.1 copy-start.6
  297.5 2.1 copy-start.9
  297.5 2.1 copy-start.21
  299.6 2.0 copy-start.2
  346.1 2.5 copy-start.18
  348.6 7.7 %copy-start.3 = (bf16[2048,256]{1,0:T(8,128)(2,1)S(1)}, bf16[2048,256]{1,0:T(8,128)(2,1)}, u32[]{:S(2)}) copy-start(bf16[2048,256]{1,0:T(8,128)(2,1)} %copy-done.2) | copy-start | bytes 3145732
  352.3 14.6 %all-to-all-start.2 = ((bf16[32,16,256]{2,1,0:T(8,128)(2,1)}), bf16[32,16,256]{2,1,0:T(8,128)(2,1)}, u32[]{:S(2)}, u32[]{:S(2)}) async-start(bf16[32,16,256]{2,1,0:T(8,128)(2,1)} %bitcast.10), calls=%async_computation.2 | async-start | bytes 524288 | tf_op jit(solution)/shard_map/all_to_all | solution.py:96
  356.3 206.0 %all-reduce.4.cloned.1.call-start = ((), (), s32[]{:S(2)}) async-start(), calls=%async_computation.3 | async-start | bytes 1245184
  370.1 6.1 %copy-start.13 = (bf16[5120]{0:T(1024)(128)(2,1)S(1)}, bf16[5120]{0:T(1024)(128)(2,1)}, u32[]{:S(2)}) copy-start(bf16[5120]{0:T(1024)(128)(2,1)} %reshape.115) | copy-start | bytes 30724
  376.3 37.6 %copy-start.5 = (bf16[2048,172]{0,1:T(8,128)(2,1)S(1)}, bf16[2048,172]{0,1:T(8,128)(2,1)}, u32[]{:S(2)}) copy-start(bf16[2048,172]{0,1:T(8,128)(2,1)} %copy-done.4) | copy-start | bytes 2113540
  376.3 37.6 %copy-start.8 = (bf16[256,172]{1,0:T(8,128)(2,1)S(1)}, bf16[256,172]{1,0:T(8,128)(2,1)}, u32[]{:S(2)}) copy-start(bf16[256,172]{1,0:T(8,128)(2,1)} %copy-done.7) | copy-start | bytes 264196
  428.0 1.8 copy-start.19
  429.4 132.9 %copy-start.12 = (f32[4864]{0:T(1024)S(1)}, f32[4864]{0:T(1024)}, u32[]{:S(2)}) copy-start(f32[4864]{0:T(1024)} %param.23) | copy-start | bytes 58372
  429.4 132.9 %copy-start.16 = (f32[4864]{0:T(1024)S(1)}, f32[4864]{0:T(1024)}, u32[]{:S(2)}) copy-start(f32[4864]{0:T(1024)} %param.24) | copy-start | bytes 58372
  429.4 132.9 %copy-start.17 = (f32[4864]{0:T(1024)S(1)}, f32[4864]{0:T(1024)}, u32[]{:S(2)}) copy-start(f32[4864]{0:T(1024)} %param.25) | copy-start | bytes 58372
  (2 other events, 1.6 us)
Sparse Core Ops, SparseCore 0:
  435.4 126.8 all-reduce.3
where the time goes:
time: 582 us; the launch traced here: 572 us
  local copies, waits for them, and re-layouts  178 us (31%)
  waiting for transfers between devices  140 us (24%)
  other arithmetic  96.4 us (17%)
  blocking collectives  84.5 us (15%)
  matrix products  41.4 us (7%)
  between operations  18.7 us (3%)
  starting transfers between devices  14 us (2%)
    gather x4, local copies, waits for them, and re-layouts, partial_sums(): picked = source_rows[jnp.maximum(sources, 0)]  148 us
    unnamed x2, waiting for transfers between devices  126 us
    all_gather x1, blocking collectives, body(): lax.all_gather(master.astype(jnp.bfloat16), 'dom', axis=0, tiled=True)  45.8 us
    psum x1, blocking collectives, body(): lax.psum((jnp.sum(row_loss * valid_mask), seed_count[0].astype(jnp.float3...  38.7 us
    scatter-add x1, other arithmetic, body(): jax.ops.segment_sum(spread, jnp.maximum(sources_two, 0).reshape(-1), MID)  37.6 us
    scatter-add x2, other arithmetic, neighbour_sums(): totals = jax.ops.segment_sum(received.astype(jnp.float32), targets, groups)  18.9 us
    scatter-add x2, other arithmetic, neighbour_sums(): jax.ops.segment_sum(counts, targets, groups)  15 us
    mul x4, local copies, waits for them, and re-layouts, body(): present_two[:, :, None] * slot_grads[:, None, :]  11.9 us
  transfers between devices with their start and end apart: 4, of which 3 were waited for; matrix products, arithmetic and copies ran while one was open for 6% of the time, Pallas kernels for 0%

commit v1 on v0

v1 whole, which is shorter than its diff:
```python
import jax
import jax.numpy as jnp
from jax import lax
from jax.experimental import pallas as pl
from jax.experimental.pallas import tpu as pltpu
from jax.sharding import PartitionSpec as P

F = 128
H = 256
C = 172
STEP = 4
SEEDS = 2048
MID = 8192
CAP1 = 64
CAP2 = 16
LIVE1 = 32
LIVE2 = 8
FAN1 = 15
FAN2 = 10
L = 128
ROWS1 = 2 * F * H // L
ROWS2 = 2 * H * C // L
BIAS = ROWS1 + ROWS2
LEAD = 8

learn_rate = 0.02
weight_decay = 0.01
adam_eps = 1e-08
f32 = jnp.float32
bf16 = jnp.bfloat16
i32 = jnp.int32
VM = pl.BlockSpec(memory_space=pltpu.VMEM)
SM = pl.BlockSpec(memory_space=pltpu.SMEM)


def params(limit=48):
    return pltpu.CompilerParams(vmem_limit_bytes=limit * 2**20)


def cost(flops, nbytes):
    return pl.CostEstimate(flops=int(flops), bytes_accessed=int(nbytes), transcendentals=0)


def nn(a, b):
    return lax.dot_general(a, b, (((1,), (0,)), ((), ())), preferred_element_type=f32)


def nt(a, b):
    return lax.dot_general(a, b, (((1,), (1,)), ((), ())), preferred_element_type=f32)


def tn(a, b):
    return lax.dot_general(a, b, (((0,), (0,)), ((), ())), preferred_element_type=f32)


def iota(shape, dim, dtype=i32):
    return lax.broadcasted_iota(i32, shape, dim).astype(dtype)


def live_key(live, cap, keep):
    row = iota((256, 256), 0)
    col = iota((256, 256), 1)
    before = ((row < col) & (row // cap == col // cap)).astype(f32).astype(bf16)
    place = nn(live.astype(f32).astype(bf16), before)
    group = iota(live.shape, 1) // cap
    return jnp.where(live, place + (group * keep).astype(f32), -1.0)


def pick_matrix(key_row):
    return (key_row == iota((L, 256), 0, f32)).astype(f32).astype(bf16)


def split_pick(value, pick):
    hi = lax.shift_right_logical(value, 6)
    lo = lax.bitwise_and(value, 63)
    both = jnp.concatenate([hi, lo], axis=0).astype(f32).astype(bf16)
    got = nt(both, pick)
    n = value.shape[0]
    return got[:n] * 64.0 + got[n:]


def rows256(ref, g):
    return jnp.concatenate([ref[2 * g : 2 * g + 1, :], ref[2 * g + 1 : 2 * g + 2, :]], axis=1)


def stack256(ref, groups):
    return jnp.concatenate([rows256(ref, g) for g in range(groups)], axis=0)


def source_tables(src_ref, fan, cap, keep, offset, groups):
    live = jnp.concatenate([src_ref[0:1, 256 * g : 256 * g + 256] for g in range(groups)], axis=0) >= 0
    key = live_key(live, cap, keep)
    tables = []
    for g in range(groups):
        pick = pick_matrix(key[g : g + 1])
        block = src_ref[:, 256 * g : 256 * g + 256]
        block = jnp.where(block >= 0, block + offset, 0)
        block = jnp.concatenate([block, jnp.zeros((16 - fan, 256), i32)], axis=0)
        tables.append(split_pick(block, pick))
    return tables


def target_tables(cnt_ref, dst_ref, cap, keep, groups, dst_out, cnt_out):
    cnt = stack256(cnt_ref, groups)
    key = live_key(cnt > 0, cap, keep)
    for g in range(groups):
        pick = pick_matrix(key[g : g + 1])
        dst = jnp.broadcast_to(rows256(dst_ref, g), (8, 256))
        dst_out[:, L * g : L * g + L] = split_pick(dst, pick)
        reps = jnp.broadcast_to(cnt[g : g + 1].astype(f32), (L, 256)).astype(bf16)
        cnt_out[L * g : L * g + L, :] = nt(pick, reps).astype(bf16)


def prep_sources(src1_ref, src2_ref, idx_out, idx2_out):
    g1 = src1_ref.shape[1] // 256
    g2 = src2_ref.shape[1] // 256
    for g, t in enumerate(source_tables(src1_ref, FAN1, CAP1, LIVE1, LEAD, g1)):
        t = t.astype(i32)
        idx_out[:, L * g : L * g + L] = t[0:8] + t[8:16] * 65536
    for g, t in enumerate(source_tables(src2_ref, FAN2, CAP2, LIVE2, 1, g2)):
        idx2_out[:, L * g : L * g + L] = t - 1.0


def prep_targets(cnt1_ref, dst1_ref, cnt2_ref, dst2_ref, d1_out, c1_out, d2_out, c2_out):
    g1 = cnt1_ref.shape[0] // 2
    g2 = cnt2_ref.shape[0] // 2
    target_tables(cnt1_ref, dst1_ref, CAP1, LIVE1, g1, d1_out, c1_out)
    target_tables(cnt2_ref, dst2_ref, CAP2, LIVE2, g2, d2_out, c2_out)


def weight_rows(master_ref, count_ref, out_ref):
    rows = master_ref.shape[0]
    out_ref[...] = jnp.zeros(out_ref.shape, bf16)
    seeds = count_ref[0]
    hi = lax.shift_right_logical(seeds, 4).astype(f32)
    lo = lax.bitwise_and(seeds, 15).astype(f32)
    lane = iota((1, L), 1)
    extra = jnp.where(lane == 0, hi, jnp.where(lane == 1, lo, 0.0))
    block = jnp.concatenate([master_ref[...], extra], axis=0).astype(bf16)
    for d in range(out_ref.shape[0]):
        out_ref[d, 0 : rows + 1, :] = block


def gather_sums(idx_ref, feat_ref, out_ref, table, hold):
    table[0:LEAD, :] = jnp.zeros((LEAD, F), f32)

    def widen(i, carry):
        at = pl.multiple_of(i * 512, 512)
        table[pl.ds(at + LEAD, 512), :] = feat_ref[pl.ds(at, 512), :].astype(f32)
        return carry

    lax.fori_loop(0, MID // 512, widen, 0)

    def sixteen(i, carry):
        at = pl.multiple_of(i * 16, 16)
        for u in range(16):
            picked = []
            for j in range(8):
                word = idx_ref[j, at + u]
                picked.append(table[pl.ds(lax.bitwise_and(word, 65535), 1), :])
                if j < 7:
                    picked.append(table[pl.ds(lax.shift_right_logical(word, 16), 1), :])
            while len(picked) > 1:
                picked = [a + b for a, b in zip(picked[::2], picked[1::2])] + picked[len(picked) // 2 * 2 :]
            hold[u : u + 1, :] = picked[0]
        out_ref[pl.ds(at, 16), :] = hold[...].astype(bf16)
        return carry

    lax.fori_loop(0, out_ref.shape[0] // 16, sixteen, 0)


def roll_left(x, r):
    return pltpu.roll(x, L - r, 1) if r else x


def unpack(rows, got_ref, w1_ref, b1_ref, w2_ref, b2_ref, total_ref, flat, left, right):
    devices = got_ref.shape[0]
    lane = iota((1, L), 1)
    seeds = jnp.zeros((1, L), f32)
    for d in range(devices):
        flat[d * rows : d * rows + rows, :] = got_ref[d, 0:rows, :].astype(f32)
        seeds = seeds + got_ref[d, rows : rows + 1, :].astype(f32)
    weight = jnp.where(lane == 0, 16.0, jnp.where(lane == 1, 1.0, 0.0))
    total = jnp.sum(seeds * weight, axis=1, keepdims=True)
    total_ref[...] = jnp.broadcast_to(total, total_ref.shape)
    w1_ref[:, 0:L] = flat[pl.ds(0, 256, stride=2), :].astype(bf16)
    w1_ref[:, L : 2 * L] = flat[pl.ds(1, 256, stride=2), :].astype(bf16)
    lanes = iota((16, L), 1)
    for i in range(32):
        q, r = divmod(C * i, L)
        one = roll_left(flat[pl.ds(ROWS1 + q, 16, stride=43), :], r)
        two = roll_left(flat[pl.ds(ROWS1 + q + 1, 16, stride=43), :], r)
        left[pl.ds(i, 16, stride=32), :] = jnp.where(lanes < L - r, one, two) if r else one
        tail = two
        if r + C - L > L:
            three = roll_left(flat[pl.ds(ROWS1 + q + 2, 16, stride=43), :], r)
            tail = jnp.where(lanes < L - r, two, three)
        right[pl.ds(i, 16, stride=32), :] = jnp.where(lanes < C - L, tail, 0.0)
    w2_ref[:, 0:L] = left[...].astype(bf16)
    w2_ref[:, L : 2 * L] = right[...].astype(bf16)
    b1 = jnp.concatenate([flat[BIAS : BIAS + 1, :], flat[BIAS + 1 : BIAS + 2, :]], axis=1)
    b1_ref[...] = jnp.broadcast_to(b1, b1_ref.shape)
    tail = jnp.where(lane < C - L, flat[BIAS + 3 : BIAS + 4, :], 0.0)
    b2 = jnp.concatenate([flat[BIAS + 2 : BIAS + 3, :], tail], axis=1)
    b2_ref[...] = jnp.broadcast_to(b2, b2_ref.shape)


def one_hot(row, start, count):
    near = (row - start.astype(f32)).astype(bf16)
    return (near == iota((count, row.shape[1]), 0, f32).astype(bf16)).astype(f32).astype(bf16)


def source_counts(idx_ref, start, count):
    total = one_hot(idx_ref[0:1, :], start, count)
    for j in range(1, FAN2):
        total = total + one_hot(idx_ref[j : j + 1, :], start, count)
    return total


def first_layer(
    feat_ref, sums_ref, cnt_ref, dst_ref, idx2_ref, w1_ref, b1_ref, pair_ref, act_ref, spread_ref, part_ref, right, acc
):
    step = pl.program_id(0)
    block = feat_ref.shape[0]

    @pl.when(step == 0)
    def _():
        right[:, 0:F] = sums_ref[...]
        right[:, F : 2 * F] = cnt_ref[...]
        acc[...] = jnp.zeros(acc.shape, f32)

    for k in range(block // 256):
        start = step * block + k * 256
        here = slice(k * 256, k * 256 + 256)
        got = nn(one_hot(dst_ref[0:1, :], start, 256), right[...])
        mean = (got[:, 0:F] / jnp.maximum(got[:, F : 2 * F], 1.0)).astype(bf16)
        pair = jnp.concatenate([feat_ref[here, :], mean], axis=1)
        pair_ref[here, :] = pair
        act = jnp.maximum(nn(pair, w1_ref[...]) + b1_ref[0:1, :], 0.0).astype(bf16)
        act_ref[here, :] = act
        spread = source_counts(idx2_ref, start, 256)
        spread_ref[here, :] = spread
        acc[...] += tn(spread, act)

    @pl.when(step == pl.num_programs(0) - 1)
    def _():
        part_ref[...] = acc[...].astype(bf16)


def second_layer(
    live_ref, labels_ref, act_ref, part_ref, cnt_ref, dst_ref, w2_ref, b2_ref, total_ref,
    ret_ref, grad_ref, mean_ref, loss_ref, acc, right,
):
    right[:, 0:H] = part_ref[...]
    right[:, H : H + L] = cnt_ref[...]
    acc[...] = jnp.zeros(acc.shape, f32)
    lane = iota((256, H), 1)
    real = lane < C
    total = total_ref[0:1, 0:1]
    loss = jnp.zeros((1, 1), f32)
    for k in range(SEEDS // 256):
        here = slice(k * 256, k * 256 + 256)
        hot = one_hot(dst_ref[0:1, :], jnp.int32(k * 256), 256)
        got = nn(hot, right[...])
        degree = jnp.maximum(got[:, H : H + L], 1.0)
        degree = jnp.concatenate([degree, degree], axis=1)
        mean = (got[:, 0:H] / degree).astype(bf16)
        mean_ref[here, :] = mean
        logits = nn(act_ref[here, :], w2_ref[0:H, :]) + nn(mean, w2_ref[H : 2 * H, :]) + b2_ref[0:1, :]
        top = jnp.max(jnp.where(real, logits, -3e38), axis=1, keepdims=True)
        raised = jnp.where(real, jnp.exp(jnp.where(real, logits - top, 0.0)), 0.0)
        norm = jnp.sum(raised, axis=1, keepdims=True)
        label = jnp.transpose(jnp.broadcast_to(rows256(labels_ref, k).astype(f32), (8, 256)))[:, 0:1]
        target = jnp.where(lane.astype(f32) == label, 1.0, 0.0)
        valid = (iota((256, 1), 0) + k * 256 < live_ref[0]).astype(f32)
        ce = (
            top + jnp.log(norm)
            - 0.9 * jnp.sum(logits * target, axis=1, keepdims=True)
            - 0.1 * (jnp.sum(jnp.where(real, logits, 0.0), axis=1, keepdims=True) / C)
        )
        loss = loss + jnp.sum(ce * valid, axis=0, keepdims=True)
        grad = jnp.where(real, (raised / norm - 0.9 * target - 0.1 / C) * (valid / total), 0.0).astype(bf16)
        grad_ref[here, :] = grad
        back = (nt(grad, w2_ref[H : 2 * H, :]) / degree).astype(bf16)
        acc[...] += tn(hot, back)
    ret_ref[...] = acc[...].astype(bf16)
    loss_ref[...] = jnp.broadcast_to(loss, loss_ref.shape)


def second_grads(act_ref, mean_ref, grad_ref, w2_ref, self_ref, flat_ref, left, right):
    grad = grad_ref[...]
    for part, rows in ((0, act_ref), (1, mean_ref)):
        got = tn(rows[...], grad)
        left[part * H : part * H + H, :] = got[:, 0:L]
        right[part * H : part * H + H, :] = got[:, L : 2 * L]
    self_ref[...] = nt(grad, w2_ref[0:H, :])
    lanes = iota((16, L), 1)
    for m in range(43):
        i, c = divmod(L * m, C)
        a0 = roll_left(left[pl.ds(i, 16, stride=32), :], c) if c < L else None
        a1 = roll_left(right[pl.ds(i, 16, stride=32), :], c % L)
        piece = a1 if a0 is None else (jnp.where(lanes < L - c, a0, a1) if c else a0)
        held = C - c
        if held < L:
            nxt = left[pl.ds(i + 1, 16, stride=32), :]
            piece = jnp.where(lanes < held, piece, pltpu.roll(nxt, held, 1) if held else nxt)
        flat_ref[pl.ds(m, 16, stride=43), :] = piece
    bias = jnp.sum(grad.astype(f32), axis=0, keepdims=True)
    flat_ref[ROWS2 : ROWS2 + 1, :] = bias[:, 0:L]
    flat_ref[ROWS2 + 1 : ROWS2 + 2, :] = bias[:, L : 2 * L]
    flat_ref[ROWS2 + 2 :, :] = jnp.zeros((flat_ref.shape[0] - ROWS2 - 2, L), f32)


def first_grads(
    rows, pair_ref, act_ref, spread_ref, slot_ref, self_ref, flat2_ref, loss_ref, out_ref, acc, bias, flat
):
    step = pl.program_id(0)
    block = pair_ref.shape[0]

    @pl.when(step == 0)
    def _():
        acc[...] = jnp.zeros(acc.shape, f32)
        bias[...] = jnp.zeros(bias.shape, f32)

    seeded = jnp.where(step * block < SEEDS, 1.0, 0.0)
    d_act = nn(spread_ref[...], slot_ref[...]) + self_ref[...] * seeded
    d_act = jnp.where(act_ref[...].astype(f32) > 0, d_act.astype(bf16).astype(f32), 0.0)
    bias[...] += jnp.sum(d_act.reshape(block // 8, 8, H), axis=0)
    acc[...] += tn(pair_ref[...], d_act.astype(bf16))

    @pl.when(step == pl.num_programs(0) - 1)
    def _():
        flat[pl.ds(0, 256, stride=2), :] = acc[:, 0:L]
        flat[pl.ds(1, 256, stride=2), :] = acc[:, L : 2 * L]
        flat[ROWS1:BIAS, :] = flat2_ref[0:ROWS2, :]
        b1 = jnp.sum(bias[...], axis=0, keepdims=True)
        flat[BIAS : BIAS + 1, :] = b1[:, 0:L]
        flat[BIAS + 1 : BIAS + 2, :] = b1[:, L : 2 * L]
        flat[BIAS + 2 : BIAS + 4, :] = flat2_ref[ROWS2 : ROWS2 + 2, :]
        flat[BIAS + 4 :, :] = jnp.zeros((flat.shape[0] - BIAS - 4, L), f32)
        spare = out_ref.shape[1] - rows
        for d in range(out_ref.shape[0]):
            out_ref[d, 0:rows, :] = flat[d * rows : d * rows + rows, :]
            out_ref[d, rows:, :] = loss_ref[0:spare, :]


def adamw(rows, got_ref, total_ref, master_ref, m1_ref, m2_ref, loss_ref, new_ref, n1_ref, n2_ref):
    total = jnp.sum(got_ref[...], axis=0)
    grad = total[0:rows]
    loss_ref[...] = total[rows : rows + 1] / total_ref[0:1, :]
    first = 0.5 * m1_ref[...] + 0.5 * grad
    second = 0.5 * m2_ref[...] + 0.5 * grad * grad
    fix = 1.0 - 0.5**STEP
    master = master_ref[...]
    n1_ref[...] = first
    n2_ref[...] = second
    new_ref[...] = master - learn_rate * (
        first / fix / (jnp.sqrt(second / fix) + adam_eps) + weight_decay * master
    )


def ceil_to(n, k):
    return -(-n // k) * k


def exchange(x):
    return lax.all_to_all(x, "dom", split_axis=0, concat_axis=0, tiled=True)


def body(features, labels, seed_count, src1, cnt1, dst1, src2, cnt2, dst2, master, moment1, moment2):
    devices = lax.axis_size("dom")
    rows = master.shape[0] // L
    n1 = devices * LIVE1
    n2 = devices * LIVE2
    send_rows = ceil_to(rows + 1, 16)
    back_rows = ceil_to(rows + 1, 8)
    S = jax.ShapeDtypeStruct
    call = pl.pallas_call
    master2 = master.reshape(rows, L)
    w_send = call(
        weight_rows, out_shape=S((devices, send_rows, L), bf16), in_specs=[VM, SM], out_specs=VM,
        compiler_params=params(), name="weight_rows",
    )(master2, seed_count)
    w_got = exchange(w_send)
    idx1, idx2 = call(
        prep_sources, out_shape=(S((8, n1), i32), S((16, n2), f32)), in_specs=[VM, VM], out_specs=(VM, VM),
        compiler_params=params(), name="prep_sources", cost_estimate=cost(1e7, 2e5),
    )(src1.T, src2.T)
    sums = call(
        gather_sums, out_shape=S((n1, F), bf16), in_specs=[SM, VM], out_specs=VM,
        scratch_shapes=[pltpu.VMEM((MID + LEAD, F), f32), pltpu.VMEM((16, F), f32)],
        compiler_params=params(), name="gather_sums", cost_estimate=cost(2e9, 4e7),
    )(idx1, features)
    got1 = exchange(sums.reshape(devices, LIVE1, F)).reshape(n1, F)
    dst1c, cnt1c, dst2c, cnt2c = call(
        prep_targets,
        out_shape=(S((8, n1), f32), S((n1, L), bf16), S((8, n2), f32), S((n2, L), bf16)),
        in_specs=[VM] * 4, out_specs=(VM,) * 4, compiler_params=params(), name="prep_targets",
        cost_estimate=cost(1e7, 4e5),
    )(*(a.reshape(-1, L) for a in (cnt1, dst1, cnt2, dst2)))
    w1, b1, w2, b2, total = call(
        lambda *refs: unpack(rows, *refs),
        out_shape=(S((256, H), bf16), S((8, H), f32), S((2 * H, H), bf16), S((8, H), f32), S((8, L), f32)),
        in_specs=[VM], out_specs=(VM,) * 5,
        scratch_shapes=[pltpu.VMEM((devices * rows, L), f32), pltpu.VMEM((2 * H, L), f32), pltpu.VMEM((2 * H, L), f32)],
        compiler_params=params(), name="unpack", cost_estimate=cost(1e7, 1e6),
    )(w_got)
    block = 1024
    steps = MID // block
    whole = lambda *shape: pl.BlockSpec(shape, lambda i: (0,) * len(shape))
    part = lambda width: pl.BlockSpec((block, width), lambda i: (i, 0))
    pair, act, spread, part2 = call(
        first_layer, grid=(steps,),
        out_shape=(S((MID, 2 * F), bf16), S((MID, H), bf16), S((MID, n2), bf16), S((n2, H), bf16)),
        in_specs=[part(F), whole(n1, F), whole(n1, L), whole(8, n1), whole(16, n2), whole(2 * F, H), whole(8, H)],
        out_specs=(part(2 * F), part(H), part(n2), whole(n2, H)),
        scratch_shapes=[pltpu.VMEM((n1, 2 * F), bf16), pltpu.VMEM((n2, H), f32)],
        compiler_params=params(), name="first_layer", cost_estimate=cost(8e9, 2e7),
    )(features, got1, cnt1c, dst1c, idx2, w1, b1)
    got2 = exchange(part2.reshape(devices, LIVE2, H)).reshape(n2, H)
    seeds_only = pl.BlockSpec((SEEDS, H), lambda i: (0, 0))
    ret, grad, mean2, loss = call(
        second_layer, grid=(1,),
        out_shape=(S((n2, H), bf16), S((SEEDS, H), bf16), S((SEEDS, H), bf16), S((8, L), f32)),
        in_specs=[SM, whole(SEEDS // L, L), seeds_only, whole(n2, H), whole(n2, L), whole(8, n2), whole(2 * H, H),
                  whole(8, H), whole(8, L)],
        out_specs=(whole(n2, H), whole(SEEDS, H), whole(SEEDS, H), whole(8, L)),
        scratch_shapes=[pltpu.VMEM((n2, H), f32), pltpu.VMEM((n2, H + L), bf16)],
        compiler_params=params(), name="second_layer", cost_estimate=cost(4e9, 5e6),
    )(seed_count, labels.reshape(-1, L), act, got2, cnt2c, dst2c, w2, b2, total)
    slot = exchange(ret.reshape(devices, LIVE2, H)).reshape(n2, H)
    from_self, flat2 = call(
        second_grads, grid=(1,), out_shape=(S((SEEDS, H), f32), S((ROWS2 + 16, L), f32)),
        in_specs=[seeds_only, whole(SEEDS, H), whole(SEEDS, H), whole(2 * H, H)],
        out_specs=(whole(SEEDS, H), whole(ROWS2 + 16, L)),
        scratch_shapes=[pltpu.VMEM((2 * H, L), f32), pltpu.VMEM((2 * H, L), f32)],
        compiler_params=params(), name="second_grads", cost_estimate=cost(4e9, 5e6),
    )(act, mean2, grad, w2)
    last = SEEDS // block - 1
    out = call(
        lambda *refs: first_grads(rows, *refs), grid=(steps,), out_shape=S((devices, back_rows, L), f32),
        in_specs=[part(2 * F), part(H), part(n2), whole(n2, H),
                  pl.BlockSpec((block, H), lambda i: (jnp.minimum(i, last), 0)), whole(ROWS2 + 16, L), whole(8, L)],
        out_specs=whole(devices, back_rows, L),
        scratch_shapes=[pltpu.VMEM((2 * F, H), f32), pltpu.VMEM((8, H), f32), pltpu.VMEM((devices * rows, L), f32)],
        compiler_params=params(), name="first_grads", cost_estimate=cost(4e9, 1e7),
    )(pair, act, spread, slot, from_self, flat2, loss)
    got3 = exchange(out)
    vec = S((rows, L), f32)
    loss_row, new_master, new_first, new_second = call(
        lambda *refs: adamw(rows, *refs), out_shape=(S((1, L), f32), vec, vec, vec), in_specs=[VM] * 5,
        out_specs=(VM,) * 4, compiler_params=params(), name="adamw",
    )(got3, total, master2, moment1.reshape(rows, L), moment2.reshape(rows, L))
    return (loss_row[0, 0], new_master.reshape(-1), new_first.reshape(-1), new_second.reshape(-1))


def solution(mesh):
    placed = (
        P("dom", None),
        P("dom"),
        P("dom"),
        P("dom", None),
        P("dom"),
        P("dom"),
        P("dom", None),
        P("dom"),
        P("dom"),
        P("dom"),
        P("dom"),
        P("dom"),
    )
    return jax.shard_map(
        body,
        mesh=mesh,
        in_specs=placed,
        out_specs=(P(), P("dom"), P("dom"), P("dom")),
        check_vma=False,
    )
```

time: 582 us -> 145 us (0.25); the launches traced: 572 us -> 144 us
  local copies, waits for them, and re-layouts: 178 us -> 10 us
  waiting for transfers between devices: 140 us -> 12.5 us
  other arithmetic: 96.4 us -> 0 us
  Pallas kernels: 0 us -> 73.9 us
  blocking collectives: 84.5 us -> 30.7 us
  matrix products: 41.4 us -> 0 us
  between operations: 18.7 us -> 1.42 us
    gather x5 -> x0, local copies, waits for them, and re-layouts: 151 us -> none  [the longest x4 148 us: partial_sums(): picked = source_rows[jnp.maximum(sources, 0)]]
    unnamed x2 -> x0, waiting for transfers between devices: 126 us -> none
    pallas_call x0 -> x10, Pallas kernels: none -> 73.9 us  [the longest x1 32.4 us: body(): call(first_layer, grid=(steps,), out_shape=(S((MID, 2 * F), bf16), S((MID...]
    scatter-add x5 -> x0, other arithmetic: 71.5 us -> none  [the longest x1 37.6 us: body(): jax.ops.segment_sum(spread, jnp.maximum(sources_two, 0).reshape(-1), MID)]
    all_gather x1 -> x0, blocking collectives: 45.8 us -> none  [body(): lax.all_gather(master.astype(jnp.bfloat16), 'dom', axis=0, tiled=True)]
    dot_general x12 -> x0, matrix products: 41.4 us -> none  [the longest x1 10 us: body(): jnp.dot(means_one, w_first[1], preferred_element_type=jnp.float32)]
    psum x1 -> x0, blocking collectives: 38.7 us -> none  [body(): lax.psum((jnp.sum(row_loss * valid_mask), seed_count[0].astype(jnp.float3...]
    all_to_all x0 -> x2, blocking collectives: none -> 30.7 us  [exchange(): return lax.all_to_all(x, 'dom', split_axis=0, concat_axis=0, tiled=True)]
  transfers between devices with their start and end apart: 4 -> 3, of which waited for: 3 -> 2; matrix products, arithmetic and copies ran while one was open for 6% -> 0% of each run, Pallas kernels for 0% -> 16%
where the time goes in v1:
time: 145 us; the launch traced here: 144 us
  Pallas kernels  73.9 us (51%)
  blocking collectives  30.7 us (21%)
  starting transfers between devices  15.7 us (11%)
  waiting for transfers between devices  12.5 us (9%)
  local copies, waits for them, and re-layouts  10 us (7%)
    pallas_call x1, Pallas kernels, body(): call(first_layer, grid=(steps,), out_shape=(S((MID, 2 * F), bf16), S((MID...  32.4 us
    all_to_all x2, blocking collectives, exchange(): return lax.all_to_all(x, 'dom', split_axis=0, concat_axis=0, tiled=True)  30.7 us
    pallas_call x1, Pallas kernels, body(): call(gather_sums, out_shape=S((n1, F), bf16), in_specs=[SM, VM], out_spec...  18 us
    all_to_all x3, starting transfers between devices, exchange(): return lax.all_to_all(x, 'dom', split_axis=0, concat_axis=0, tiled=True)  15.7 us
    all_to_all x3, waiting for transfers between devices, exchange(): return lax.all_to_all(x, 'dom', split_axis=0, concat_axis=0, tiled=True)  12.5 us
    unnamed x34, local copies, waits for them, and re-layouts  10 us
    pallas_call x1, Pallas kernels, body(): call(lambda *refs: first_grads(rows, *refs), grid=(steps,), out_shape=S((...  9.01 us
    pallas_call x1, Pallas kernels, body(): call(second_layer, grid=(1,), out_shape=(S((n2, H), bf16), S((SEEDS, H),...  8.61 us
  transfers between devices with their start and end apart: 3, of which 2 were waited for; matrix products, arithmetic and copies ran while one was open for 0% of the time, Pallas kernels for 16%

profile of v1, /device:TPU:0, one launch (start us, length us, event | category | flops | bytes accessed | tf_op | source)
XLA Modules:
  0.0 144.3 jit_solution(13106547338502364903)
XLA Ops:
  1.3 0.7 copy-done.1
  2.0 0.8 weight_rows.1
  2.9 7.3 %all-to-all-start.1 = ((bf16[32,48,128]{2,1,0:T(8,128)(2,1)}), bf16[32,48,128]{2,1,0:T(8,128)(2,1)S(1)}, u32[]{:S(2)}, u32[]{:S(2)}) async-start(bf16[32,48,128]{2,1,0:T(8,128)(2,1)} %weight_rows.1), calls=%async_computation.1 | async-start | bytes 786432 | tf_op jit(solution)/shard_map/all_to_all | solution.py:367
  10.2 0.9 copy-done
  11.1 0.8 copy-done.3
  12.5 1.6 %copy-done.6 = bf16[8192,128]{1,0:T(8,128)(2,1)S(1)} copy-done((bf16[8192,128]{1,0:T(8,128)(2,1)S(1)}, bf16[8192,128]{1,0:T(8,128)(2,1)}, u32[]{:S(2)}) %copy-start.6) | copy-done | bytes 2097176
  14.1 18.0 %gather_sums.1 = bf16[1024,128]{1,0:T(8,128)(2,1)} custom-call(s32[8,1024]{1,0:T(8,128)S(1)} %get-tuple-element.29.idx_ref, bf16[8192,128]{1,0:T(8,128)(2,1)S(1)} %copy-done.6), custom_call_target="tpu_custom_call" | custom-call | flops 2000000000 | bytes 40000000 | tf_op jit(solution)/shard_map/gather_sums/pallas_call | solution.py:389
  32.1 5.8 %all-to-all-start = ((bf16[32,32,128]{2,1,0:T(8,128)(2,1)}), bf16[32,32,128]{2,1,0:T(8,128)(2,1)S(1)}, u32[]{:S(2)}, u32[]{:S(2)}) async-start(bf16[32,32,128]{2,1,0:T(8,128)(2,1)} %bitcast.2), calls=%async_computation | async-start | bytes 524288 | tf_op jit(solution)/shard_map/all_to_all | solution.py:367
  38.0 0.8 prep_targets.1
  39.4 9.1 %all-to-all-done = bf16[32,32,128]{2,1,0:T(8,128)(2,1)S(1)} async-done(((bf16[32,32,128]{2,1,0:T(8,128)(2,1)}), bf16[32,32,128]{2,1,0:T(8,128)(2,1)S(1)}, u32[]{:S(2)}, u32[]{:S(2)}) %all-to-all-start) | async-done | bytes 262176 | tf_op jit(solution)/shard_map/all_to_all | solution.py:367
  48.5 1.6 %copy-done.7 = bf16[8192,128]{1,0:T(8,128)(2,1)S(1)} copy-done((bf16[8192,128]{1,0:T(8,128)(2,1)S(1)}, bf16[8192,128]{1,0:T(8,128)(2,1)}, u32[]{:S(2)}) %copy-start.7) | copy-done | bytes 2097176
  50.1 32.4 %first_layer.1 = (bf16[8192,256]{1,0:T(8,128)(2,1)}, bf16[8192,256]{1,0:T(8,128)(2,1)}, bf16[8192,256]{1,0:T(8,128)(2,1)}, bf16[256,256]{1,0:T(8,128)(2,1)S(1)}) custom-call(bf16[8192,128]{1,0:T(8,128)(2,1)S(1)} %copy-done.7, bf16[1024,128]{1,0:T(8,128)(2,1)S(1)} %bitcast.22, bf16[1024,128]{1,0:T(8,128)(2,1)S(1)} %get-tuple-element.30.cnt_ref, ...), custom_call_target="tpu_custom_call" | custom-call | flops 8000000000 | bytes 20000000 | tf_op jit(solution)/shard_map/first_layer/pallas_call | solution.py:412
  82.5 10.4 %all_to_all.25 = bf16[32,8,256]{2,1,0:T(8,128)(2,1)S(1)} all-to-all(bf16[32,8,256]{2,1,0:T(8,128)(2,1)S(1)} %bitcast.25), channel_id=1, replica_groups=mesh['dom'=32] {'dom'}, dimensions={0} | all-to-all | bytes 262144 | tf_op jit(solution)/shard_map/all_to_all | solution.py:367
  92.9 8.6 %second_layer.1 = (bf16[256,256]{1,0:T(8,128)(2,1)}, bf16[2048,256]{1,0:T(8,128)(2,1)S(1)}, bf16[2048,256]{1,0:T(8,128)(2,1)S(1)}, f32[8,128]{1,0:T(8,128)S(1)}) custom-call(s32[1]{0:T(128)S(6)} %copy.16.count_ref.live_ref, s32[16,128]{1,0:T(8,128)S(1)} %bitcast.33, bf16[8192,256]{1,0:T(8,128)(2,1)} %get-tuple-element.36.act_ref.refs_1_, ...), custom_call_target="tpu_custom_call" | custom-call | flops 4000000000 | bytes 5000000 | tf_op jit(solution)/shard_map/second_layer/pallas_call | solution.py:422
  101.5 1.0 copy-done.13
  102.5 1.0 copy-done.15
  103.5 2.6 %all-to-all-start.3 = ((bf16[32,8,256]{2,1,0:T(8,128)(2,1)}), bf16[32,8,256]{2,1,0:T(8,128)(2,1)S(1)}, u32[]{:S(2)}, u32[]{:S(2)}) async-start(bf16[32,8,256]{2,1,0:T(8,128)(2,1)} %bitcast.12), calls=%async_computation.3 | async-start | bytes 262144 | tf_op jit(solution)/shard_map/all_to_all | solution.py:367
  106.1 1.2 copy-done.14
  107.3 1.2 copy-done.16
  108.5 2.4 %second_grads.1 = (f32[2048,256]{1,0:T(8,128)S(1)}, f32[704,128]{1,0:T(8,128)S(1)}) custom-call(bf16[8192,256]{1,0:T(8,128)(2,1)} %get-tuple-element.36.act_ref.refs_1_, bf16[2048,256]{1,0:T(8,128)(2,1)S(1)} %copy-done.16, bf16[2048,256]{1,0:T(8,128)(2,1)S(1)} %copy-done.14, bf16[512,256]{1,0:T(8,128)(2,1)S(1)} %get-tuple-element.41.w2_ref), custom_call_target="tpu_custom_call" | custom-call | flops 4000000000 | bytes 5000000 | tf_op jit(solution)/shard_map/second_grads/pallas_call | solution.py:432
  110.9 3.3 %all-to-all-done.3 = bf16[32,8,256]{2,1,0:T(8,128)(2,1)S(1)} async-done(((bf16[32,8,256]{2,1,0:T(8,128)(2,1)}), bf16[32,8,256]{2,1,0:T(8,128)(2,1)S(1)}, u32[]{:S(2)}, u32[]{:S(2)}) %all-to-all-start.3) | async-done | bytes 131104 | tf_op jit(solution)/shard_map/all_to_all | solution.py:367
  114.3 9.0 %first_grads.1 = f32[32,40,128]{2,1,0:T(8,128)S(1)} custom-call(bf16[8192,256]{1,0:T(8,128)(2,1)} %get-tuple-element.35.refs_0_, bf16[8192,256]{1,0:T(8,128)(2,1)} %get-tuple-element.36.act_ref.refs_1_, bf16[8192,256]{1,0:T(8,128)(2,1)} %get-tuple-element.37.refs_2_, bf16[256,256]{1,0:T(8,128)(2,1)S(1)} %bitcast.21, ...), custom_call_target="tpu_custom_call" | custom-call | flops 4000000000 | bytes 10000000 | tf_op jit(solution)/shard_map/first_grads/pallas_call | solution.py:440
  123.3 20.3 %all_to_all.26.refs_0_ = f32[32,40,128]{2,1,0:T(8,128)S(1)} all-to-all(f32[32,40,128]{2,1,0:T(8,128)S(1)} %first_grads.1), channel_id=1, replica_groups=mesh['dom'=32] {'dom'}, dimensions={0} | all-to-all | bytes 1310720 | tf_op jit(solution)/shard_map/all_to_all | solution.py:367
  143.6 0.7 adamw.1
  (28 shorter events, 1.3 us)
Async XLA Ops:
  1.3 0.7 copy-start.1
  2.9 35.1 %copy-start.8 = (s32[2048]{0:T(1024)S(1)}, s32[2048]{0:T(1024)}, u32[]{:S(2)}) copy-start(s32[2048]{0:T(1024)} %param.16) | copy-start | bytes 24580
  2.9 35.1 %copy-start.9 = (s32[2048]{0:T(1024)S(1)}, s32[2048]{0:T(1024)}, u32[]{:S(2)}) copy-start(s32[2048]{0:T(1024)} %param.17) | copy-start | bytes 24580
  2.9 35.1 %copy-start.12 = (s32[512]{0:T(512)S(1)}, s32[512]{0:T(512)}, u32[]{:S(2)}) copy-start(s32[512]{0:T(512)} %param.20) | copy-start | bytes 6148
  2.9 29.2 %all-to-all-start.1 = ((bf16[32,48,128]{2,1,0:T(8,128)(2,1)}), bf16[32,48,128]{2,1,0:T(8,128)(2,1)S(1)}, u32[]{:S(2)}, u32[]{:S(2)}) async-start(bf16[32,48,128]{2,1,0:T(8,128)(2,1)} %weight_rows.1), calls=%async_computation.1 | async-start | bytes 786432 | tf_op jit(solution)/shard_map/all_to_all | solution.py:367
  10.2 27.8 %copy-start.11 = (s32[512]{0:T(512)S(1)}, s32[512]{0:T(512)}, u32[]{:S(2)}) copy-start(s32[512]{0:T(512)} %param.19) | copy-start | bytes 6148
  10.2 0.9 copy-start
  11.1 0.8 copy-start.3
  12.5 1.6 %copy-start.6 = (bf16[8192,128]{1,0:T(8,128)(2,1)S(1)}, bf16[8192,128]{1,0:T(8,128)(2,1)}, u32[]{:S(2)}) copy-start(bf16[8192,128]{1,0:T(8,128)(2,1)} %feat_ref.3) | copy-start | bytes 6291460
  32.1 16.4 %all-to-all-start = ((bf16[32,32,128]{2,1,0:T(8,128)(2,1)}), bf16[32,32,128]{2,1,0:T(8,128)(2,1)S(1)}, u32[]{:S(2)}, u32[]{:S(2)}) async-start(bf16[32,32,128]{2,1,0:T(8,128)(2,1)} %bitcast.2), calls=%async_computation | async-start | bytes 524288 | tf_op jit(solution)/shard_map/all_to_all | solution.py:367
  48.5 1.6 %copy-start.7 = (bf16[8192,128]{1,0:T(8,128)(2,1)S(1)}, bf16[8192,128]{1,0:T(8,128)(2,1)}, u32[]{:S(2)}) copy-start(bf16[8192,128]{1,0:T(8,128)(2,1)} %feat_ref.3) | copy-start | bytes 6291460
  50.1 42.8 %copy-start.10 = (s32[2048]{0:T(1024)S(1)}, s32[2048]{0:T(1024)}, u32[]{:S(2)}) copy-start(s32[2048]{0:T(1024)} %param.13) | copy-start | bytes 24580
  101.5 1.0 copy-start.13
  102.5 1.0 copy-start.15
  103.5 10.8 %all-to-all-start.3 = ((bf16[32,8,256]{2,1,0:T(8,128)(2,1)}), bf16[32,8,256]{2,1,0:T(8,128)(2,1)S(1)}, u32[]{:S(2)}, u32[]{:S(2)}) async-start(bf16[32,8,256]{2,1,0:T(8,128)(2,1)} %bitcast.12), calls=%async_computation.3 | async-start | bytes 262144 | tf_op jit(solution)/shard_map/all_to_all | solution.py:367
  106.1 1.2 copy-start.14
  107.3 1.2 copy-start.16
  114.3 29.3 %copy-start.2 = (f32[4864]{0:T(1024)S(1)}, f32[4864]{0:T(1024)}, u32[]{:S(2)}) copy-start(f32[4864]{0:T(1024)} %param.21) | copy-start | bytes 58372
  114.3 29.3 %copy-start.4 = (f32[4864]{0:T(1024)S(1)}, f32[4864]{0:T(1024)}, u32[]{:S(2)}) copy-start(f32[4864]{0:T(1024)} %param.22) | copy-start | bytes 58372
  114.3 29.3 %copy-start.5 = (f32[4864]{0:T(1024)S(1)}, f32[4864]{0:T(1024)}, u32[]{:S(2)}) copy-start(f32[4864]{0:T(1024)} %param.23) | copy-start | bytes 58372
